TPU v7x, 256 devices: a whole 4x4x8 slice. The times are simulated.
256 devices in a mesh: dp: 4 (over x), seq: 8 (over z_lo, y), tensor: 8 (over z_hi, core).
Axes of the slice: x: 4, y: 4, z: 8 (z_hi: 4, z_lo: 2; z = z_hi * 2 + z_lo), core: 2. Of those that a mesh axis runs over, the one named last changes fastest.
Arguments:
- hidden: bfloat16 [4096, 28672], P(('dp', 'seq'), 'tensor'), may hold values from -6 to 6
- weight: bfloat16 [28672, 4096], P('tensor', 'seq'), may hold values from -0.03125 to 0.03125
- out_grad: bfloat16 [4096, 4096], P(('dp', 'tensor'), 'seq'), may hold values from -6 to 6
Outputs:
- output: bfloat16 [4096, 4096], P(('dp', 'tensor'), 'seq')
- grad_hidden: bfloat16 [4096, 28672], P(('dp', 'seq'), 'tensor')
- grad_weight: bfloat16 [28672, 4096], P('tensor', 'seq')
All inputs are finite; a program needn't handle non-finite values.
Results may differ from a plain program's by a relative error of at most 0.017.
Values may be sent and summed in bfloat16 or wider, within the bound.
A program may use at most 128 MiB of HBM per device.

v0:
```python
import jax
import jax.numpy as jnp
from jax import lax
from jax.sharding import PartitionSpec as P

HB = 512


def partner_2(shard, axis, distance):
    return lax.ppermute(shard, axis, [(i, i ^ 1 << distance) for i in range(lax.axis_size(axis))])


def walsh_table(table_order):
    matrix = jnp.ones((1, 1), jnp.float32)
    while matrix.shape[0] < table_order:
        matrix = jnp.concatenate(
            [jnp.concatenate([matrix, matrix], 1), jnp.concatenate([matrix, -matrix], 1)], 0
        )
    return matrix


def local_blocks(values, inner_table):
    row_count, feature_count = values.shape
    block_size = inner_table.shape[0]
    shaped = values.reshape(row_count, feature_count // block_size, block_size)
    if values.dtype == jnp.bfloat16:
        mixed_rows = jnp.einsum(
            "rbk,kl->rbl",
            shaped,
            inner_table.astype(jnp.bfloat16),
            preferred_element_type=jnp.float32,
        )
    else:
        mixed_rows = jnp.einsum("rbk,kl->rbl", shaped, inner_table, precision=lax.Precision.HIGHEST)
    return mixed_rows.reshape(row_count, feature_count)


def butterfly(values):
    axis_count = lax.axis_size("tensor")
    device_index = lax.axis_index("tensor")
    for bit_index in range(axis_count.bit_length() - 1):
        partner = partner_2(values.astype(jnp.bfloat16), "tensor", bit_index).astype(values.dtype)
        upper_half = device_index // (1 << bit_index) % 2 == 1
        values = jnp.where(upper_half, partner - values, values + partner)
    return values


def rotate(values, inner_table, norm_scale):
    return (butterfly(local_blocks(values, inner_table)) * norm_scale).astype(jnp.bfloat16)


def body(hidden, weight, out_grad):
    inner_table = walsh_table(HB)
    norm_scale = 1.0 / float(lax.axis_size("tensor") * HB) ** 0.5
    rotated = rotate(hidden, inner_table, norm_scale)
    gathered = lax.all_gather(rotated, "seq", axis=0, tiled=True)
    partial_sums = jnp.dot(gathered, weight, preferred_element_type=jnp.float32)
    output = lax.psum_scatter(
        partial_sums.astype(jnp.bfloat16), "tensor", scatter_dimension=0, tiled=True
    )
    grads_all = lax.all_gather(out_grad, "tensor", axis=0, tiled=True)
    token_total = hidden.shape[0] * lax.axis_size("seq") * lax.axis_size("dp")
    grad_term = lax.dot_general(
        gathered, grads_all, (((0,), (0,)), ((), ())), preferred_element_type=jnp.float32
    )
    grad_weight = lax.psum(
        (grad_term * (1.0 / float(token_total) ** 0.5)).astype(jnp.bfloat16), "dp"
    )
    rotated_grad = lax.psum_scatter(
        lax.dot_general(
            grads_all, weight, (((1,), (1,)), ((), ())), preferred_element_type=jnp.float32
        ).astype(jnp.bfloat16),
        "seq",
        scatter_dimension=0,
        tiled=True,
    ).astype(jnp.float32)
    grad_hidden = rotate(rotated_grad, inner_table, norm_scale)
    return (output, grad_hidden, grad_weight)


def solution(mesh):
    in_specs = (P(("dp", "seq"), "tensor"), P("tensor", "seq"), P(("dp", "tensor"), "seq"))
    out_specs = (P(("dp", "tensor"), "seq"), P(("dp", "seq"), "tensor"), P("tensor", "seq"))
    return jax.shard_map(body, mesh=mesh, in_specs=in_specs, out_specs=out_specs, check_vma=False)
```

profile of v0, /device:TPU:1, one launch (start us, length us, event | category | flops | bytes accessed | tf_op | source)
XLA Modules:
  0.0 447.1 jit_solution(14021014759159372248)
XLA Ops:
  7.2 0.7 all-gather.5.cloned.1.call-update
  7.9 36.3 %all-gather.5.cloned.1.call-done = bf16[1024,512]{1,0:T(8,128)(2,1)} async-done(((bf16[128,512]{1,0:T(8,128)(2,1)}), bf16[1024,512]{1,0:T(8,128)(2,1)}) %all-gather.5.cloned.1.call-update) | async-done | bytes 1048592 | tf_op jit(solution)/shard_map/all_gather | solution.py:61
  44.2 9.3 %convolution_convert_fusion = bf16[1024,3584]{1,0:T(8,128)(2,1)} fusion(bf16[1024,512]{1,0:T(8,128)(2,1)} %all-gather.5.cloned.1.call-done, bf16[3584,512]{1,0:T(8,128)(2,1)} %param.4), kind=kOutput, calls=%fused_computation | convolution fusion | flops 3761766400 | bytes 12058624 | tf_op jit(solution)/shard_map/dot_general | solution.py:70
  53.6 1.1 copy-done
  54.7 0.6 copy.11
  55.3 0.7 fusion.14
  56.0 1.0 bitcast_convert_fusion.1
  57.4 2.4 collective-permute-done
  59.7 1.2 fusion.13
  61.0 1.6 collective-permute-start.1
  62.5 41.3 %collective-permute-done.1 = bf16[128,3584]{0,1:T(8,128)(2,1)} collective-permute-done((bf16[128,3584]{0,1:T(8,128)(2,1)}, bf16[128,3584]{0,1:T(8,128)(2,1)}, u32[]{:S(2)}, u32[]{:S(2)}) %collective-permute-start.1) | collective-permute-done | bytes 917536 | tf_op jit(solution)/shard_map/ppermute | solution.py:10
  103.8 2.6 fusion.11
  106.5 2.7 collective-permute-start.2
  109.2 62.5 %collective-permute-done.2 = bf16[128,3584]{0,1:T(8,128)(2,1)} collective-permute-done((bf16[128,3584]{0,1:T(8,128)(2,1)}, bf16[128,3584]{0,1:T(8,128)(2,1)}, u32[]{:S(2)}, u32[]{:S(2)}) %collective-permute-start.2) | collective-permute-done | bytes 917536 | tf_op jit(solution)/shard_map/ppermute | solution.py:10
  171.7 3.2 fusion.4
  175.0 20.5 %reduce-scatter.5.cloned.1.call-done = bf16[128,3584]{1,0:T(8,128)(2,1)} async-done(((bf16[1024,3584]{1,0:T(8,128)(2,1)}), bf16[128,3584]{1,0:T(8,128)(2,1)}) %reduce-scatter.5.cloned.1.call-update) | async-done | bytes 917520 | tf_op jit(solution)/shard_map/reduce_scatter | solution.py:69
  195.5 1.5 copy.13
  197.0 3.1 fusion.15
  200.1 1.0 bitcast_convert_fusion
  201.5 79.5 %all-gather.3.cloned.1.call-done = bf16[1024,3584]{0,1:T(8,128)(2,1)} async-done(((bf16[128,3584]{0,1:T(8,128)(2,1)}), bf16[1024,3584]{0,1:T(8,128)(2,1)}) %all-gather.3.cloned.1.call-update) | async-done | bytes 7340048 | tf_op jit(solution)/shard_map/all_gather | solution.py:56
  281.0 9.1 %convolution_convert_fusion.1 = bf16[1024,512]{1,0:T(8,128)(2,1)} fusion(bf16[1024,3584]{0,1:T(8,128)(2,1)} %all-gather.3.cloned.1.call-done, bf16[3584,512]{1,0:T(8,128)(2,1)} %param.4), kind=kOutput, calls=%fused_computation.26 | convolution fusion | flops 3758620672 | bytes 12058624 | tf_op jit(solution)/shard_map/dot_general | solution.py:57
  290.2 1.2 fusion.12
  291.4 2.3 collective-permute-start.4
  293.7 8.5 %multiply_convert_fusion = bf16[3584,512]{1,0:T(8,128)(2,1)} fusion(bf16[1024,3584]{0,1:T(8,128)(2,1)} %all-gather.3.cloned.1.call-done, bf16[1024,512]{1,0:T(8,128)(2,1)S(1)} %copy-done.2), kind=kOutput, calls=%fused_computation.1 | convolution fusion | flops 3761766400 | bytes 12058624 | tf_op jit(solution)/shard_map/dot_general | solution.py:63
  302.2 41.2 %collective-permute-done.4 = bf16[128,3584]{0,1:T(8,128)(2,1)} collective-permute-done((bf16[128,3584]{0,1:T(8,128)(2,1)}, bf16[128,3584]{0,1:T(8,128)(2,1)}, u32[]{:S(2)}, u32[]{:S(2)}) %collective-permute-start.4) | collective-permute-done | bytes 917536 | tf_op jit(solution)/shard_map/ppermute | solution.py:10
  343.4 1.7 fusion.10
  345.1 6.5 %collective-permute-start.5 = (bf16[128,3584]{0,1:T(8,128)(2,1)S(1)}, bf16[128,3584]{0,1:T(8,128)(2,1)S(1)}, u32[]{:S(2)}, u32[]{:S(2)}) collective-permute-start(bf16[128,3584]{0,1:T(8,128)(2,1)S(1)} %fusion.10), channel_id=1, source_target_pairs={{0,4},{1,5},{2,6},{3,7},{4,0},{5,1},{6,2},{7,3},{8,12},{9,13},{10,... | collective-permute-start | bytes 2752520 | tf_op jit(solution)/shard_map/ppermute | solution.py:10
  351.6 40.0 %collective-permute-done.5 = bf16[128,3584]{0,1:T(8,128)(2,1)S(1)} collective-permute-done((bf16[128,3584]{0,1:T(8,128)(2,1)S(1)}, bf16[128,3584]{0,1:T(8,128)(2,1)S(1)}, u32[]{:S(2)}, u32[]{:S(2)}) %collective-permute-start.5) | collective-permute-done | bytes 917536 | tf_op jit(solution)/shard_map/ppermute | solution.py:10
  391.6 3.0 fusion.9
  394.6 2.2 copy.16
  396.8 39.6 %all-reduce.2.cloned.1.call-done = bf16[3584,512]{1,0:T(8,128)(2,1)} async-done(((bf16[3584,512]{1,0:T(8,128)(2,1)}), bf16[3584,512]{1,0:T(8,128)(2,1)}) %all-reduce.2.cloned.1.call-update) | async-done | bytes 3670032 | tf_op jit(solution)/shard_map/psum | solution.py:66
  436.4 4.1 copy.21
  (18 shorter events, 1.0 us)
Async XLA Ops:
  7.2 37.1 %all-gather.5.cloned.1.call-start = ((), (), s32[]{:S(2)}) async-start(), calls=%async_computation.4 | async-start | bytes 1179648 | tf_op jit(solution)/shard_map/all_gather | solution.py:61
  7.9 187.6 %reduce-scatter.5.cloned.1.call-start = ((), (), s32[]{:S(2)}) async-start(), calls=%async_computation.5 | async-start | bytes 8257536 | tf_op jit(solution)/shard_map/reduce_scatter | solution.py:69
  53.5 1.2 copy-start
  53.6 1.8 copy-start.1
  53.6 227.5 %all-gather.3.cloned.1.call-start = ((), (), s32[]{:S(2)}) async-start(), calls=%async_computation.2 | async-start | bytes 8257536 | tf_op jit(solution)/shard_map/all_gather | solution.py:56
  57.1 2.7 collective-permute-start
  61.0 42.9 %collective-permute-start.1 = (bf16[128,3584]{0,1:T(8,128)(2,1)}, bf16[128,3584]{0,1:T(8,128)(2,1)}, u32[]{:S(2)}, u32[]{:S(2)}) collective-permute-start(bf16[128,3584]{0,1:T(8,128)(2,1)} %fusion.13), channel_id=1, source_target_pairs={{0,2},{1,3},{2,0},{3,1},{4,6},{5,7},{6,4},{7,5},{8,10},{9,11},{10,... | collective-permute-start | bytes 2752520 | tf_op jit(solution)/shard_map/ppermute | solution.py:10
  106.5 65.2 %collective-permute-start.2 = (bf16[128,3584]{0,1:T(8,128)(2,1)}, bf16[128,3584]{0,1:T(8,128)(2,1)}, u32[]{:S(2)}, u32[]{:S(2)}) collective-permute-start(bf16[128,3584]{0,1:T(8,128)(2,1)} %fusion.11), channel_id=1, source_target_pairs={{0,4},{1,5},{2,6},{3,7},{4,0},{5,1},{6,2},{7,3},{8,12},{9,13},{10,... | collective-permute-start | bytes 2752520 | tf_op jit(solution)/shard_map/ppermute | solution.py:10
  175.0 221.8 %reduce-scatter.3.cloned.1.call-start = ((), (), s32[]{:S(2)}) async-start(), calls=%async_computation.3 | async-start | bytes 1179648 | tf_op jit(solution)/shard_map/reduce_scatter | solution.py:58
  201.1 89.1 %collective-permute-start.3 = (bf16[128,3584]{0,1:T(8,128)(2,1)}, bf16[128,3584]{0,1:T(8,128)(2,1)S(1)}, u32[]{:S(2)}, u32[]{:S(2)}) collective-permute-start(bf16[128,3584]{0,1:T(8,128)(2,1)} %bitcast_convert_fusion), channel_id=1, source_target_pairs={{0,1},{1,0},{2,3},{3,2},{4,5},{5,4},{6,7},{7,6},{8,9},{9,8},{10,11... | collective-permute-start | bytes 2752520 | tf_op jit(solution)/shard_map/ppermute | solution.py:10
  290.1 146.3 %all-reduce.2.cloned.1.call-start = ((), (), s32[]{:S(2)}) async-start(), calls=%async_computation.6 | async-start | bytes 7340032 | tf_op jit(solution)/shard_map/psum | solution.py:66
  290.2 3.5 copy-start.2
  291.4 52.0 %collective-permute-start.4 = (bf16[128,3584]{0,1:T(8,128)(2,1)}, bf16[128,3584]{0,1:T(8,128)(2,1)}, u32[]{:S(2)}, u32[]{:S(2)}) collective-permute-start(bf16[128,3584]{0,1:T(8,128)(2,1)} %fusion.12), channel_id=1, source_target_pairs={{0,2},{1,3},{2,0},{3,1},{4,6},{5,7},{6,4},{7,5},{8,10},{9,11},{10,... | collective-permute-start | bytes 2752520 | tf_op jit(solution)/shard_map/ppermute | solution.py:10
  345.1 46.4 %collective-permute-start.5 = (bf16[128,3584]{0,1:T(8,128)(2,1)S(1)}, bf16[128,3584]{0,1:T(8,128)(2,1)S(1)}, u32[]{:S(2)}, u32[]{:S(2)}) collective-permute-start(bf16[128,3584]{0,1:T(8,128)(2,1)S(1)} %fusion.10), channel_id=1, source_target_pairs={{0,4},{1,5},{2,6},{3,7},{4,0},{5,1},{6,2},{7,3},{8,12},{9,13},{10,... | collective-permute-start | bytes 2752520 | tf_op jit(solution)/shard_map/ppermute | solution.py:10
Sparse Core Ops, SparseCore 0:
  9.8 34.3 all-gather.4
  53.7 141.7 reduce-scatter.4
  197.8 83.2 all-gather.2
  290.3 50.2 reduce-scatter.2
  343.4 93.0 all-reduce.1
where the time goes:
time: 447 us
  waiting for transfers between devices  364 us (81%)
  matrix products  30.6 us (7%)
  other arithmetic  15 us (3%)
  starting transfers between devices  13.9 us (3%)
  between operations  13.8 us (3%)
  local copies, waits for them, and re-layouts  9.58 us (2%)
    ppermute x6, waiting for transfers between devices, partner_2(): lax.ppermute(shard, axis, [(i, i ^ 1 << distance) for i in range(lax.axis...  187 us
    all_gather x1, waiting for transfers between devices, body(): gathered = lax.all_gather(rotated, 'seq', axis=0, tiled=True)  79.5 us
    psum x1, waiting for transfers between devices, body(): lax.psum((grad_term * (1.0 / float(token_total) ** 0.5)).astype(jnp.bfloa...  39.6 us
    all_gather x1, waiting for transfers between devices, body(): grads_all = lax.all_gather(out_grad, 'tensor', axis=0, tiled=True)  36.3 us
    reduce_scatter x1, waiting for transfers between devices, body(): lax.psum_scatter(lax.dot_general(grads_all, weight, (((1,), (1,)), ((), (...  20.5 us
    ppermute x6, starting transfers between devices, partner_2(): lax.ppermute(shard, axis, [(i, i ^ 1 << distance) for i in range(lax.axis...  13.7 us
    dot_general x1, matrix products, body(): lax.dot_general(grads_all, weight, (((1,), (1,)), ((), ())), preferred_el...  9.3 us
    dot_general x1, matrix products, body(): partial_sums = jnp.dot(gathered, weight, preferred_element_type=jnp.float32)  9.08 us
  transfers between devices with their start and end apart: 11, of which 9 were waited for; matrix products, arithmetic and copies ran while one was open for 9% of the time, Pallas kernels for 0%

commit v1 on v0

v1 whole, which is shorter than its diff:
```python
import jax
import jax.numpy as jnp
from jax import lax
from jax.experimental import pallas as pl
from jax.experimental.pallas import tpu as pltpu
from jax.sharding import PartitionSpec as P

HB = 512
NB = 7
BF = jnp.bfloat16
F32 = jnp.float32
MESH = pl.DeviceIdType.MESH
STAGES = ("f1", "g", "f2", "f3l", "f3r", "f4", "x1", "x2", "b1l", "b1r", "b2", "b3", "b4", "o")


def parity_table():
    row = lax.broadcasted_iota(jnp.int32, (HB, HB), 0)
    col = lax.broadcasted_iota(jnp.int32, (HB, HB), 1)
    both = row & col
    both = both ^ (both >> 8)
    both = both ^ (both >> 4)
    both = both ^ (both >> 2)
    both = both ^ (both >> 1)
    return jnp.where((both & 1) == 1, -1.0, 1.0).astype(BF)


def walsh8(parts):
    for bit in (1, 2, 4):
        parts = [
            parts[i] + parts[i ^ bit] if i & bit == 0 else parts[i ^ bit] - parts[i]
            for i in range(8)
        ]
    return parts


def kernel(hid, wgt, ogr, out, ghid, gwgt, a, r, hg, p, q1, q2, s, z, t2, d, xr, dd, gv, wv, oa, op, orx, tab, recv, send, wsem):
    x = lax.axis_index("dp")
    sq = lax.axis_index("seq")
    tn = lax.axis_index("tensor")
    zl = sq // 4
    y = sq % 4
    yr = (y + 1) % 4
    yl = (y + 3) % 4
    yo = (y + 2) % 4
    right = (x, zl * 4 + yr, tn)
    left = (x, zl * 4 + yl, tn)

    def R(name, j):
        return recv.at[STAGES.index(name), j]

    def S(name, j):
        return send.at[STAGES.index(name), j]

    def rows(n):
        return wv.at[pl.ds(0, n)]

    def wait(sem, n):
        pltpu.make_async_copy(rows(n), rows(n), sem).wait()

    def put(src, dst, name, j, dev, sname=None):
        pltpu.make_async_remote_copy(
            src_ref=src, dst_ref=dst, send_sem=S(sname or name, j), recv_sem=R(name, j),
            device_id=dev, device_id_type=MESH,
        ).start()

    def local(src, dst, name, j):
        pltpu.make_async_copy(src, dst, R(name, j)).start()

    def cols(j):
        return pl.ds(pl.multiple_of(j * HB, HB), HB)

    def r16(i):
        return pl.ds(pl.multiple_of(i * 16, 16), 16)

    wcopy = pltpu.make_async_copy(wgt, wv, wsem)
    wcopy.start()

    bar = pltpu.get_barrier_semaphore()
    peers = [(x, sq, (tn + k) % 8) for k in range(1, 8)]
    peers += [(x, (sq + 4) % 8, (tn + k) % 8) for k in range(8)]
    peers += [right, left]
    peers += [((x + k) % 4, sq, tn) for k in range(1, 4)]
    for dev in peers:
        pl.semaphore_signal(bar, inc=1, device_id=dev, device_id_type=MESH)
    pl.semaphore_wait(bar, len(peers))

    def f1(j):
        for k in range(1, 8):
            to = (tn + k) % 8
            put(hid.at[r16(to), cols(j)], a.at[j, tn], "f1", j, (x, sq, to))
        local(hid.at[r16(tn), cols(j)], a.at[j, tn], "f1", j)

    f1(0)
    for k in range(1, 8):
        put(ogr, gv.at[tn], "g", 0, (x, sq, (tn + k) % 8))
    local(ogr, gv.at[tn], "g", 0)

    @pl.loop(1, NB)
    def _(j):
        f1(j)

    tab[...] = parity_table()
    oa[...] = jnp.zeros_like(oa)

    def rotate_to(mixed, dst, j):
        parts = walsh8([mixed[i * 16:(i + 1) * 16] for i in range(8)])
        for i in range(8):
            dst[j, i] = (parts[i] * (1.0 / 64.0)).astype(BF)

    def spread(src, dst, name, j):
        for zk in range(2):
            zt = (zl + zk) % 2
            for k in range(8):
                to = (tn + k) % 8
                if zk == 0 and k == 0:
                    local(src(zl, tn), dst, name, j)
                else:
                    put(src(zt, to), dst, name, j, (x, zt * 4 + y, to))

    def f2(j):
        wait(R("f1", j), 128)
        mixed = jnp.dot(a[j].reshape(128, HB), tab[...], preferred_element_type=F32)
        rotate_to(mixed, r, j)
        spread(lambda zt, to: r.at[j, to], hg.at[j, zl, y, tn], "f2", j)

    def f3(j):
        wait(R("f2", j), 256)
        put(hg.at[j, :, y], hg.at[j, :, y], "f3l", j, right)
        put(hg.at[j, :, y], hg.at[j, :, y], "f3r", j, left)

    def f4(j):
        wait(R("f3l", j), 256)
        put(hg.at[j, 0, yl], hg.at[j, 0, yl], "f4", j, right)
        wait(R("f3r", j), 256)
        put(hg.at[j, 1, yr], hg.at[j, 1, yr], "f4", j, left)

    def wj(j):
        return wv[pl.ds(pl.multiple_of(j * HB, HB), HB), :]

    def f5(j):
        wait(R("f4", j), 256)
        whole = hg[j].reshape(1024, HB)
        grad = lax.dot_general(
            whole, gv[...].reshape(1024, HB), (((0,), (0,)), ((), ())), preferred_element_type=F32
        )
        d[j] = (grad * (1.0 / 64.0)).astype(BF).reshape(4, 128, HB)
        for k in range(1, 4):
            to = (x + k) % 4
            put(d.at[j, to], xr.at[j, k - 1], "x1", j, (to, sq, tn))
        oa[...] += jnp.dot(whole, wj(j), preferred_element_type=F32)

    def x2(j):
        wait(R("x1", j), 384)
        total = d[j, x].astype(F32)
        for k in range(3):
            total = total + xr[j, k].astype(F32)
        dd[j] = total.astype(BF)
        mine = gwgt.at[pl.ds(pl.multiple_of(j * HB + x * 128, 128), 128)]
        for k in range(1, 4):
            put(dd.at[j], mine, "x2", j, ((x + k) % 4, sq, tn))
        local(dd.at[j], mine, "x2", j)

    def b1(j):
        part = lax.dot_general(
            gv[...].reshape(1024, HB), wj(j), (((1,), (1,)), ((), ())), preferred_element_type=F32
        )
        p[j] = part.astype(BF).reshape(2, 4, 128, HB)
        put(p.at[j, 0, yo], q1.at[j, 0], "b1l", j, right)
        put(p.at[j, 1, yo], q1.at[j, 1], "b1r", j, left)

    def b2(j):
        wait(R("b1l", j), 128)
        p[j, 0, yr] = (p[j, 0, yr].astype(F32) + q1[j, 0].astype(F32)).astype(BF)
        put(p.at[j, :, yr], q2.at[j, 0], "b2", j, right)
        wait(R("b1r", j), 128)
        p[j, 1, yl] = (p[j, 1, yl].astype(F32) + q1[j, 1].astype(F32)).astype(BF)
        put(p.at[j, :, yl], q2.at[j, 1], "b2", j, left)

    def b3(j):
        wait(R("b2", j), 512)
        total = p[j, :, y].astype(F32) + q2[j, 0].astype(F32) + q2[j, 1].astype(F32)
        s[j] = total.astype(BF).reshape(2, 8, 16, HB)
        spread(lambda zt, to: s.at[j, zt, to], z.at[j, zl, tn], "b3", j)

    def b4(j):
        wait(R("b3", j), 256)
        mixed = jnp.dot(z[j, 0].reshape(128, HB), tab[...], preferred_element_type=F32)
        mixed = mixed + jnp.dot(z[j, 1].reshape(128, HB), tab[...], preferred_element_type=F32)
        rotate_to(mixed, t2, j)
        mine = ghid.at[r16(tn), cols(j)]
        for k in range(1, 8):
            to = (tn + k) % 8
            put(t2.at[j, to], mine, "b4", j, (x, sq, to))
        local(t2.at[j, tn], mine, "b4", j)

    f2(0)
    wcopy.wait()
    wait(R("g", 0), 1024)

    @pl.loop(0, NB + 1)
    def _(j):
        @pl.when(j < NB)
        def _():
            f3(j)
            b1(j)

        @pl.when(j == NB)
        def _():
            op[...] = oa[...].astype(BF).reshape(8, 128, HB)
            for k in range(1, 8):
                to = (tn + k) % 8
                put(op.at[to], orx.at[k - 1], "o", 0, (x, sq, to))

        @pl.when(j >= 1)
        def _():
            b3(j - 1)

        @pl.when(j + 1 < NB)
        def _():
            f2(j + 1)

        @pl.when(j < NB)
        def _():
            f4(j)
            b2(j)

        @pl.when(j >= 1)
        def _():
            x2(j - 1)
            b4(j - 1)

        @pl.when(j < NB)
        def _():
            f5(j)

    wait(R("o", 0), 896)
    total = op[tn].astype(F32)
    for k in range(7):
        total = total + orx[k].astype(F32)
    out[...] = total.astype(BF)

    wait(S("g", 0), 896)
    wait(S("o", 0), 896)

    @pl.loop(0, NB)
    def _(j):
        wait(R("x2", j), 512)
        wait(R("b4", j), 128)
        for name, n in (("f1", 112), ("f2", 240), ("f3l", 256), ("f3r", 256), ("f4", 256), ("x1", 384),
                        ("x2", 384), ("b1l", 128), ("b1r", 128), ("b2", 512), ("b3", 240), ("b4", 112)):
            wait(S(name, j), n)


def body(hidden, weight, out_grad):
    vm = pltpu.VMEM
    ns = len(STAGES)
    return pl.pallas_call(
        kernel,
        name="rotated_projection",
        out_shape=(
            jax.ShapeDtypeStruct((128, HB), BF),
            jax.ShapeDtypeStruct((128, NB * HB), BF),
            jax.ShapeDtypeStruct((NB * HB, HB), BF),
        ),
        in_specs=[pl.BlockSpec(memory_space=pl.ANY)] * 3,
        out_specs=(
            pl.BlockSpec(memory_space=pltpu.VMEM),
            pl.BlockSpec(memory_space=pl.ANY),
            pl.BlockSpec(memory_space=pl.ANY),
        ),
        scratch_shapes=[
            vm((NB, 8, 16, HB), BF),
            vm((NB, 8, 16, HB), BF),
            vm((NB, 2, 4, 8, 16, HB), BF),
            vm((NB, 2, 4, 128, HB), BF),
            vm((NB, 2, 128, HB), BF),
            vm((NB, 2, 2, 128, HB), BF),
            vm((NB, 2, 8, 16, HB), BF),
            vm((NB, 2, 8, 16, HB), BF),
            vm((NB, 8, 16, HB), BF),
            vm((NB, 4, 128, HB), BF),
            vm((NB, 3, 128, HB), BF),
            vm((NB, 128, HB), BF),
            vm((8, 128, HB), BF),
            vm((NB * HB, HB), BF),
            vm((1024, HB), F32),
            vm((8, 128, HB), BF),
            vm((7, 128, HB), BF),
            vm((HB, HB), BF),
            pltpu.SemaphoreType.DMA((ns, NB)),
            pltpu.SemaphoreType.DMA((ns, NB)),
            pltpu.SemaphoreType.DMA,
        ],
        compiler_params=pltpu.CompilerParams(
            collective_id=0, has_side_effects=True, vmem_limit_bytes=60 * 1024 * 1024
        ),
    )(hidden, weight, out_grad)


def solution(mesh):
    in_specs = (P(("dp", "seq"), "tensor"), P("tensor", "seq"), P(("dp", "tensor"), "seq"))
    out_specs = (P(("dp", "tensor"), "seq"), P(("dp", "seq"), "tensor"), P("tensor", "seq"))
    return jax.shard_map(body, mesh=mesh, in_specs=in_specs, out_specs=out_specs, check_vma=False)
```

time: 447 us -> 228 us (0.51)
  waiting for transfers between devices: 364 us -> 0 us
  Pallas kernels: 0 us -> 219 us
  matrix products: 30.6 us -> 0 us
  other arithmetic: 15 us -> 0 us
  starting transfers between devices: 13.9 us -> 0 us
  between operations: 13.8 us -> 0.64 us
    pallas_call x0 -> x1, Pallas kernels: none -> 219 us  [body(): pl.pallas_call(kernel, name='rotated_projection', out_shape=(jax.ShapeDty...]
    ppermute x6 -> x0, waiting for transfers between devices: 187 us -> none  [partner_2(): lax.ppermute(shard, axis, [(i, i ^ 1 << distance) for i in range(lax.axis...]
    all_gather x2 -> x0, waiting for transfers between devices: 116 us -> none  [the longest x1 79.5 us: body(): gathered = lax.all_gather(rotated, 'seq', axis=0, tiled=True)]
    psum x1 -> x0, waiting for transfers between devices: 39.6 us -> none  [body(): lax.psum((grad_term * (1.0 / float(token_total) ** 0.5)).astype(jnp.bfloa...]
    dot_general x5 -> x0, matrix products: 30.6 us -> none  [the longest x1 9.3 us: body(): lax.dot_general(grads_all, weight, (((1,), (1,)), ((), ())), preferred_el...]
    reduce_scatter x2 -> x0, waiting for transfers between devices: 20.5 us -> none  [the longest x1 20.5 us: body(): lax.psum_scatter(lax.dot_general(grads_all, weight, (((1,), (1,)), ((), (...]
    convert_element_type x8 -> x0, other arithmetic: 15 us -> none  [the longest x6 8.82 us: butterfly(): values.astype(jnp.bfloat16)]
    ppermute x6 -> x0, starting transfers between devices: 13.7 us -> none  [partner_2(): lax.ppermute(shard, axis, [(i, i ^ 1 << distance) for i in range(lax.axis...]
  transfers between devices with their start and end apart: 11 -> 0, of which waited for: 9 -> 0; matrix products, arithmetic and copies ran while one was open for 9% -> 0% of each run, Pallas kernels for 0% -> 0%
where the time goes in v1:
time: 228 us; the launch traced here: 227 us
  Pallas kernels  219 us (96%)
  local copies, waits for them, and re-layouts  7.84 us (3%)
    pallas_call x1, Pallas kernels, body(): pl.pallas_call(kernel, name='rotated_projection', out_shape=(jax.ShapeDty...  219 us
    unnamed x3, local copies, waits for them, and re-layouts  7.84 us

profile of v1, /device:TPU:1, one launch (start us, length us, event | category | flops | bytes accessed | tf_op | source)
XLA Modules:
  0.0 227.5 jit_solution(2266445754245791366)
XLA Ops:
  0.6 219.0 %rotated_projection.1 = (bf16[128,512]{1,0:T(8,128)(2,1)}, bf16[128,3584]{1,0:T(8,128)(2,1)}, bf16[3584,512]{1,0:T(8,128)(2,1)}) custom-call(bf16[128,3584]{1,0:T(8,128)(2,1)} %hid.1, bf16[3584,512]{1,0:T(8,128)(2,1)} %wgt.1, bf16[128,512]{1,0:T(8,128)(2,1)} %ogr.1), custom_call_target="tpu_custom_call" | custom-call | tf_op jit(solution)/shard_map/rotated_projection/pallas_call | solution.py:257
  219.7 1.6 copy.9
  221.2 2.2 copy.10
  223.4 4.1 %copy.11 = bf16[3584,512]{1,0:T(8,128)(2,1)} copy(bf16[3584,512]{1,0:T(8,128)(2,1)} %get-tuple-element.8) | data formatting | bytes 7340032

commit v2 on v1

--- a/solution.py
+++ b/solution.py
@@ -10,7 +10,10 @@
 BF = jnp.bfloat16
 F32 = jnp.float32
 MESH = pl.DeviceIdType.MESH
-STAGES = ("f1", "g", "f2", "f3l", "f3r", "f4", "x1", "x2", "b1l", "b1r", "b2", "b3", "b4", "o")
+STAGES = (
+    "f1", "g1", "g2", "f2", "f2b", "f3l", "f3r", "f4", "x1", "x2",
+    "b1l", "b1r", "b2", "b3a", "b3", "b4", "o1", "o2",
+)
 
 
 def parity_table():
@@ -33,7 +36,7 @@
     return parts
 
 
-def kernel(hid, wgt, ogr, out, ghid, gwgt, a, r, hg, p, q1, q2, s, z, t2, d, xr, dd, gv, wv, oa, op, orx, tab, recv, send, wsem):
+def kernel(hid, wgt, ogr, out, ghid, gwgt, a, r, hg, p, q1, q2, s, zz, s2, z, t2, d, xr, dd, gv, wv, oa, op, oh, o2, orx, tab, recv, send, wsem):
     x = lax.axis_index("dp")
     sq = lax.axis_index("seq")
     tn = lax.axis_index("tensor")
@@ -44,6 +47,17 @@
     yo = (y + 2) % 4
     right = (x, zl * 4 + yr, tn)
     left = (x, zl * 4 + yl, tn)
+    zh = tn // 2
+    co = tn % 2
+    beside = (x, (1 - zl) * 4 + y, tn)
+    twin = (x, sq, zh * 2 + 1 - co)
+
+    def near_sites(lo):
+        e = (zh + 3 + 2 * lo) % 4
+        return ((0, e), (1, e), (1 - lo, (zh + 2) % 4), (lo, zh))
+
+    def near_lo(k):
+        return (zl, 0, 1 - zl, 1)[k]
 
     def R(name, j):
         return recv.at[STAGES.index(name), j]
@@ -90,15 +104,23 @@
             put(hid.at[r16(to), cols(j)], a.at[j, tn], "f1", j, (x, sq, to))
         local(hid.at[r16(tn), cols(j)], a.at[j, tn], "f1", j)
 
+    def g1(k):
+        put(ogr, gv.at[tn], "g1", 0, (x, sq, (tn + 2 * k) % 8))
+
+    def g0():
+        put(ogr, gv.at[tn], "g2", 0, twin)
+        local(ogr, gv.at[tn], "g1", 0)
+
+    def g2():
+        wait(R("g1", 0), 512)
+        for k in range(1, 4):
+            part = (tn + 2 * k) % 8
+            put(gv.at[part], gv.at[part], "g2", 0, twin)
+
     f1(0)
-    for k in range(1, 8):
-        put(ogr, gv.at[tn], "g", 0, (x, sq, (tn + k) % 8))
-    local(ogr, gv.at[tn], "g", 0)
-
-    @pl.loop(1, NB)
-    def _(j):
-        f1(j)
-
+    g0()
+    for k in (1, 3, 2):
+        g1(k)
     tab[...] = parity_table()
     oa[...] = jnp.zeros_like(oa)
 
@@ -107,24 +129,27 @@
         for i in range(8):
             dst[j, i] = (parts[i] * (1.0 / 64.0)).astype(BF)
 
-    def spread(src, dst, name, j):
-        for zk in range(2):
-            zt = (zl + zk) % 2
-            for k in range(8):
-                to = (tn + k) % 8
-                if zk == 0 and k == 0:
-                    local(src(zl, tn), dst, name, j)
-                else:
-                    put(src(zt, to), dst, name, j, (x, zt * 4 + y, to))
-
     def f2(j):
         wait(R("f1", j), 128)
         mixed = jnp.dot(a[j].reshape(128, HB), tab[...], preferred_element_type=F32)
         rotate_to(mixed, r, j)
-        spread(lambda zt, to: r.at[j, to], hg.at[j, zl, y, tn], "f2", j)
+        land = hg.at[j, zl, y, tn]
+        for k in range(4):
+            for c in range(2):
+                to = ((zh + k) % 4) * 2 + (co + c) % 2
+                if k == 0 and c == 0:
+                    local(r.at[j, tn], land, "f2", j)
+                else:
+                    put(r.at[j, to], land, "f2", j, (x, near_lo(k) * 4 + y, to))
+
+    def f2b(j):
+        wait(R("f2", j), 128)
+        for lo, hi in near_sites(zl):
+            part = hg.at[j, lo, y, pl.ds(hi * 2, 2)]
+            put(part, part, "f2b", j, beside)
 
     def f3(j):
-        wait(R("f2", j), 256)
+        wait(R("f2b", j), 128)
         put(hg.at[j, :, y], hg.at[j, :, y], "f3l", j, right)
         put(hg.at[j, :, y], hg.at[j, :, y], "f3r", j, left)
 
@@ -137,17 +162,19 @@
     def wj(j):
         return wv[pl.ds(pl.multiple_of(j * HB, HB), HB), :]
 
-    def f5(j):
+    def f5a(j):
         wait(R("f4", j), 256)
-        whole = hg[j].reshape(1024, HB)
+        oa[...] += jnp.dot(hg[j].reshape(1024, HB), wj(j), preferred_element_type=F32)
+
+    def f5b(j):
         grad = lax.dot_general(
-            whole, gv[...].reshape(1024, HB), (((0,), (0,)), ((), ())), preferred_element_type=F32
+            hg[j].reshape(1024, HB), gv[...].reshape(1024, HB), (((0,), (0,)), ((), ())),
+            preferred_element_type=F32,
         )
         d[j] = (grad * (1.0 / 64.0)).astype(BF).reshape(4, 128, HB)
         for k in range(1, 4):
             to = (x + k) % 4
             put(d.at[j, to], xr.at[j, k - 1], "x1", j, (to, sq, tn))
-        oa[...] += jnp.dot(whole, wj(j), preferred_element_type=F32)
 
     def x2(j):
         wait(R("x1", j), 384)
@@ -176,16 +203,29 @@
         p[j, 1, yl] = (p[j, 1, yl].astype(F32) + q1[j, 1].astype(F32)).astype(BF)
         put(p.at[j, :, yl], q2.at[j, 1], "b2", j, left)
 
-    def b3(j):
+    def b3a(j):
         wait(R("b2", j), 512)
         total = p[j, :, y].astype(F32) + q2[j, 0].astype(F32) + q2[j, 1].astype(F32)
         s[j] = total.astype(BF).reshape(2, 8, 16, HB)
-        spread(lambda zt, to: s.at[j, zt, to], z.at[j, zl, tn], "b3", j)
+        for i, (lo, hi) in enumerate(near_sites(1 - zl)):
+            put(s.at[j, lo, pl.ds(hi * 2, 2)], zz.at[j, i], "b3a", j, beside)
+
+    def b3(j):
+        wait(R("b3a", j), 128)
+        for i, (lo, hi) in enumerate(near_sites(zl)):
+            pair = s[j, lo, pl.ds(hi * 2, 2)].astype(F32) + zz[j, i].astype(F32)
+            s2[j, i] = pair.astype(BF)
+        for i, (lo, hi) in enumerate(near_sites(zl)):
+            for c in range(2):
+                cc = (co + c) % 2
+                if i == 3 and c == 0:
+                    local(s2.at[j, i, cc], z.at[j, tn], "b3", j)
+                else:
+                    put(s2.at[j, i, cc], z.at[j, tn], "b3", j, (x, lo * 4 + y, hi * 2 + cc))
 
     def b4(j):
-        wait(R("b3", j), 256)
-        mixed = jnp.dot(z[j, 0].reshape(128, HB), tab[...], preferred_element_type=F32)
-        mixed = mixed + jnp.dot(z[j, 1].reshape(128, HB), tab[...], preferred_element_type=F32)
+        wait(R("b3", j), 128)
+        mixed = jnp.dot(z[j].reshape(128, HB), tab[...], preferred_element_type=F32)
         rotate_to(mixed, t2, j)
         mine = ghid.at[r16(tn), cols(j)]
         for k in range(1, 8):
@@ -193,61 +233,74 @@
             put(t2.at[j, to], mine, "b4", j, (x, sq, to))
         local(t2.at[j, tn], mine, "b4", j)
 
+    def o1():
+        op[...] = oa[...].astype(BF).reshape(4, 2, 128, HB)
+        for k in range(4):
+            put(op.at[k, 1 - co], oh.at[k], "o1", 0, twin)
+
+    def o2s():
+        wait(R("o1", 0), 512)
+        for k in range(4):
+            o2[k] = (op[k, co].astype(F32) + oh[k].astype(F32)).astype(BF)
+        for k in range(1, 4):
+            to = (zh + k) % 4
+            put(o2.at[to], orx.at[k - 1], "o2", 0, (x, sq, to * 2 + co))
+
+    def at(cond, *steps):
+        @pl.when(cond)
+        def _():
+            for step in steps:
+                step()
+
     f2(0)
+    f1(1)
+    g2()
     wcopy.wait()
-    wait(R("g", 0), 1024)
-
-    @pl.loop(0, NB + 1)
+    wait(R("g2", 0), 512)
+    b1(0)
+    f2b(0)
+    f2(1)
+    f1(2)
+    f3(0)
+
+    @pl.loop(0, NB)
     def _(j):
-        @pl.when(j < NB)
-        def _():
-            f3(j)
-            b1(j)
-
-        @pl.when(j == NB)
-        def _():
-            op[...] = oa[...].astype(BF).reshape(8, 128, HB)
-            for k in range(1, 8):
-                to = (tn + k) % 8
-                put(op.at[to], orx.at[k - 1], "o", 0, (x, sq, to))
-
-        @pl.when(j >= 1)
-        def _():
-            b3(j - 1)
-
-        @pl.when(j + 1 < NB)
-        def _():
-            f2(j + 1)
-
-        @pl.when(j < NB)
-        def _():
-            f4(j)
-            b2(j)
-
-        @pl.when(j >= 1)
-        def _():
-            x2(j - 1)
-            b4(j - 1)
-
-        @pl.when(j < NB)
-        def _():
-            f5(j)
-
-    wait(R("o", 0), 896)
-    total = op[tn].astype(F32)
-    for k in range(7):
+        prev = j >= 1
+        more = j + 1 < NB
+        b2(j)
+        at(j + 3 < NB, lambda: f1(j + 3))
+        at(prev, lambda: b3a(j - 1))
+        at(j + 2 < NB, lambda: f2(j + 2))
+        f4(j)
+        at(prev, lambda: b3(j - 1))
+        at(more, lambda: b1(j + 1), lambda: f2b(j + 1), lambda: f3(j + 1))
+        at(prev, lambda: x2(j - 1))
+        at(j + 1 == NB, lambda: b3a(j))
+        f5a(j)
+        at(j + 1 == NB, o1)
+        f5b(j)
+        at(prev, lambda: b4(j - 1))
+
+    b3(NB - 1)
+    o2s()
+    x2(NB - 1)
+    b4(NB - 1)
+
+    wait(R("o2", 0), 384)
+    total = o2[zh].astype(F32)
+    for k in range(3):
         total = total + orx[k].astype(F32)
     out[...] = total.astype(BF)
 
-    wait(S("g", 0), 896)
-    wait(S("o", 0), 896)
+    for name, n in (("g1", 384), ("g2", 512), ("o1", 512), ("o2", 384)):
+        wait(S(name, 0), n)
 
     @pl.loop(0, NB)
     def _(j):
         wait(R("x2", j), 512)
         wait(R("b4", j), 128)
-        for name, n in (("f1", 112), ("f2", 240), ("f3l", 256), ("f3r", 256), ("f4", 256), ("x1", 384),
-                        ("x2", 384), ("b1l", 128), ("b1r", 128), ("b2", 512), ("b3", 240), ("b4", 112)):
+        for name, n in (("f1", 112), ("f2", 112), ("f2b", 128), ("f3l", 256), ("f3r", 256), ("f4", 256), ("x1", 384),
+                        ("x2", 384), ("b1l", 128), ("b1r", 128), ("b2", 512), ("b3a", 128), ("b3", 112), ("b4", 112)):
             wait(S(name, j), n)
 
 
@@ -258,16 +311,12 @@
         kernel,
         name="rotated_projection",
         out_shape=(
-            jax.ShapeDtypeStruct((128, HB), BF),
-            jax.ShapeDtypeStruct((128, NB * HB), BF),
-            jax.ShapeDtypeStruct((NB * HB, HB), BF),
+            pltpu.VMEM((128, HB), BF),
+            pltpu.VMEM((128, NB * HB), BF),
+            pltpu.VMEM((NB * HB, HB), BF),
         ),
         in_specs=[pl.BlockSpec(memory_space=pl.ANY)] * 3,
-        out_specs=(
-            pl.BlockSpec(memory_space=pltpu.VMEM),
-            pl.BlockSpec(memory_space=pl.ANY),
-            pl.BlockSpec(memory_space=pl.ANY),
-        ),
+        out_specs=(pl.BlockSpec(memory_space=pltpu.VMEM),) * 3,
         scratch_shapes=[
             vm((NB, 8, 16, HB), BF),
             vm((NB, 8, 16, HB), BF),
@@ -276,7 +325,9 @@
             vm((NB, 2, 128, HB), BF),
             vm((NB, 2, 2, 128, HB), BF),
             vm((NB, 2, 8, 16, HB), BF),
-            vm((NB, 2, 8, 16, HB), BF),
+            vm((NB, 4, 2, 16, HB), BF),
+            vm((NB, 4, 2, 16, HB), BF),
+            vm((NB, 8, 16, HB), BF),
             vm((NB, 8, 16, HB), BF),
             vm((NB, 4, 128, HB), BF),
             vm((NB, 3, 128, HB), BF),
@@ -284,15 +335,17 @@
             vm((8, 128, HB), BF),
             vm((NB * HB, HB), BF),
             vm((1024, HB), F32),
-            vm((8, 128, HB), BF),
-            vm((7, 128, HB), BF),
+            vm((4, 2, 128, HB), BF),
+            vm((4, 128, HB), BF),
+            vm((4, 128, HB), BF),
+            vm((3, 128, HB), BF),
             vm((HB, HB), BF),
             pltpu.SemaphoreType.DMA((ns, NB)),
             pltpu.SemaphoreType.DMA((ns, NB)),
             pltpu.SemaphoreType.DMA,
         ],
         compiler_params=pltpu.CompilerParams(
-            collective_id=0, has_side_effects=True, vmem_limit_bytes=60 * 1024 * 1024
+            collective_id=0, has_side_effects=True, vmem_limit_bytes=54 * 1024 * 1024
         ),
     )(hidden, weight, out_grad)
 

time: 228 us -> 187 us (0.82)
  Pallas kernels: 219 us -> 182 us
  local copies, waits for them, and re-layouts: 7.84 us -> 3.42 us
    pallas_call x1, Pallas kernels: 219 us -> 182 us  [body(): pl.pallas_call(kernel, name='rotated_projection', out_shape=(pltpu.VMEM((...]
    unnamed x3, local copies, waits for them, and re-layouts: 7.84 us -> 3.42 us
where the time goes in v2:
time: 187 us; the launch traced here: 186 us
  Pallas kernels  182 us (97%)
  local copies, waits for them, and re-layouts  3.42 us (2%)
    pallas_call x1, Pallas kernels, body(): pl.pallas_call(kernel, name='rotated_projection', out_shape=(pltpu.VMEM((...  182 us

profile of v2, /device:TPU:1, one launch (start us, length us, event | category | flops | bytes accessed | tf_op | source)
XLA Modules:
  0.0 186.5 jit_solution(2631841819103361110)
XLA Ops:
  0.6 182.4 %rotated_projection.1 = (bf16[128,512]{1,0:T(8,128)(2,1)S(1)}, bf16[128,3584]{1,0:T(8,128)(2,1)S(1)}, bf16[3584,512]{1,0:T(8,128)(2,1)S(1)}) custom-call(bf16[128,3584]{1,0:T(8,128)(2,1)} %hid.1, bf16[3584,512]{1,0:T(8,128)(2,1)} %wgt.1, bf16[128,512]{1,0:T(8,128)(2,1)} %ogr.1), custom_call_target="tpu_custom_call" | custom-call | tf_op jit(solution)/shard_map/rotated_projection/pallas_call | solution.py:310
  183.1 0.7 copy.9
  183.7 0.9 copy.10
  184.6 1.8 copy.11

commit v3 on v2

--- a/solution.py
+++ b/solution.py
@@ -117,10 +117,10 @@
             part = (tn + 2 * k) % 8
             put(gv.at[part], gv.at[part], "g2", 0, twin)
 
-    f1(0)
     g0()
     for k in (1, 3, 2):
         g1(k)
+    f1(0)
     tab[...] = parity_table()
     oa[...] = jnp.zeros_like(oa)
 
@@ -252,12 +252,15 @@
             for step in steps:
                 step()
 
-    f2(0)
-    f1(1)
     g2()
     wcopy.wait()
     wait(R("g2", 0), 512)
     b1(0)
+    b1(1)
+    f2(0)
+    f1(1)
+    b2(0)
+    b1(2)
     f2b(0)
     f2(1)
     f1(2)
@@ -265,26 +268,23 @@
 
     @pl.loop(0, NB)
     def _(j):
-        prev = j >= 1
         more = j + 1 < NB
-        b2(j)
+        at(more, lambda: b2(j + 1))
         at(j + 3 < NB, lambda: f1(j + 3))
-        at(prev, lambda: b3a(j - 1))
+        b3a(j)
         at(j + 2 < NB, lambda: f2(j + 2))
         f4(j)
-        at(prev, lambda: b3(j - 1))
-        at(more, lambda: b1(j + 1), lambda: f2b(j + 1), lambda: f3(j + 1))
-        at(prev, lambda: x2(j - 1))
-        at(j + 1 == NB, lambda: b3a(j))
+        b3(j)
+        at(j + 3 < NB, lambda: b1(j + 3))
+        at(more, lambda: f2b(j + 1), lambda: f3(j + 1))
+        at(j >= 1, lambda: x2(j - 1))
         f5a(j)
         at(j + 1 == NB, o1)
         f5b(j)
-        at(prev, lambda: b4(j - 1))
-
-    b3(NB - 1)
-    o2s()
+        at(j + 1 == NB, o2s)
+        b4(j)
+
     x2(NB - 1)
-    b4(NB - 1)
 
     wait(R("o2", 0), 384)
     total = o2[zh].astype(F32)

time: 187 us -> 183 us (0.979)
  Pallas kernels: 182 us -> 178 us
    pallas_call x1, Pallas kernels: 182 us -> 178 us  [body(): pl.pallas_call(kernel, name='rotated_projection', out_shape=(pltpu.VMEM((...]
where the time goes in v3:
time: 183 us; the launch traced here: 182 us
  Pallas kernels  178 us (97%)
  local copies, waits for them, and re-layouts  3.42 us (2%)
    pallas_call x1, Pallas kernels, body(): pl.pallas_call(kernel, name='rotated_projection', out_shape=(pltpu.VMEM((...  178 us

profile of v3, /device:TPU:1, one launch (start us, length us, event | category | flops | bytes accessed | tf_op | source)
XLA Modules:
  0.0 182.5 jit_solution(5701236558429959808)
XLA Ops:
  0.6 178.4 %rotated_projection.1 = (bf16[128,512]{1,0:T(8,128)(2,1)S(1)}, bf16[128,3584]{1,0:T(8,128)(2,1)S(1)}, bf16[3584,512]{1,0:T(8,128)(2,1)S(1)}) custom-call(bf16[128,3584]{1,0:T(8,128)(2,1)} %hid.1, bf16[3584,512]{1,0:T(8,128)(2,1)} %wgt.1, bf16[128,512]{1,0:T(8,128)(2,1)} %ogr.1), custom_call_target="tpu_custom_call" | custom-call | tf_op jit(solution)/shard_map/rotated_projection/pallas_call | solution.py:310
  179.1 0.7 copy.9
  179.7 0.9 copy.10
  180.6 1.8 %copy.11 = bf16[3584,512]{1,0:T(8,128)(2,1)} copy(bf16[3584,512]{1,0:T(8,128)(2,1)S(1)} %get-tuple-element.5) | data formatting | bytes 7340032

commit v4 on v3

--- a/solution.py
+++ b/solution.py
@@ -235,16 +235,17 @@
 
     def o1():
         op[...] = oa[...].astype(BF).reshape(4, 2, 128, HB)
-        for k in range(4):
-            put(op.at[k, 1 - co], oh.at[k], "o1", 0, twin)
+        for k in (2, 1, 3, 0):
+            q = (zh + k) % 4
+            put(op.at[q, 1 - co], oh.at[q], "o1", q, twin)
 
     def o2s():
-        wait(R("o1", 0), 512)
-        for k in range(4):
-            o2[k] = (op[k, co].astype(F32) + oh[k].astype(F32)).astype(BF)
-        for k in range(1, 4):
-            to = (zh + k) % 4
-            put(o2.at[to], orx.at[k - 1], "o2", 0, (x, sq, to * 2 + co))
+        for k in (2, 1, 3, 0):
+            q = (zh + k) % 4
+            wait(R("o1", q), 128)
+            o2[q] = (op[q, co].astype(F32) + oh[q].astype(F32)).astype(BF)
+            if k:
+                put(o2.at[q], orx.at[k - 1], "o2", 0, (x, sq, q * 2 + co))
 
     def at(cond, *steps):
         @pl.when(cond)
@@ -269,19 +270,21 @@
     @pl.loop(0, NB)
     def _(j):
         more = j + 1 < NB
+        last = j + 1 == NB
         at(more, lambda: b2(j + 1))
         at(j + 3 < NB, lambda: f1(j + 3))
-        b3a(j)
+        at(j == 0, lambda: b3a(j))
         at(j + 2 < NB, lambda: f2(j + 2))
+        at(last, lambda: b3(j))
         f4(j)
-        b3(j)
+        at(more, lambda: b3(j))
         at(j + 3 < NB, lambda: b1(j + 3))
-        at(more, lambda: f2b(j + 1), lambda: f3(j + 1))
-        at(j >= 1, lambda: x2(j - 1))
+        at(more, lambda: f2b(j + 1), lambda: f3(j + 1), lambda: b3a(j + 1))
+        at(jnp.logical_and(j >= 1, more), lambda: x2(j - 1))
         f5a(j)
-        at(j + 1 == NB, o1)
+        at(last, o1)
         f5b(j)
-        at(j + 1 == NB, o2s)
+        at(last, lambda: x2(j - 1), o2s)
         b4(j)
 
     x2(NB - 1)
@@ -292,8 +295,10 @@
         total = total + orx[k].astype(F32)
     out[...] = total.astype(BF)
 
-    for name, n in (("g1", 384), ("g2", 512), ("o1", 512), ("o2", 384)):
+    for name, n in (("g1", 384), ("g2", 512), ("o2", 384)):
         wait(S(name, 0), n)
+    for k in range(4):
+        wait(S("o1", k), 128)
 
     @pl.loop(0, NB)
     def _(j):

time: 183 us -> 175 us (0.956)
  Pallas kernels: 178 us -> 171 us
    pallas_call x1, Pallas kernels: 178 us -> 171 us  [body(): pl.pallas_call(kernel, name='rotated_projection', out_shape=(pltpu.VMEM((...]
where the time goes in v4:
time: 175 us
  Pallas kernels  171 us (98%)
  local copies, waits for them, and re-layouts  3.42 us (2%)
    pallas_call x1, Pallas kernels, body(): pl.pallas_call(kernel, name='rotated_projection', out_shape=(pltpu.VMEM((...  171 us

profile of v4, /device:TPU:1, one launch (start us, length us, event | category | flops | bytes accessed | tf_op | source)
XLA Modules:
  0.0 175.1 jit_solution(7065758793090762683)
XLA Ops:
  0.6 171.0 %rotated_projection.1 = (bf16[128,512]{1,0:T(8,128)(2,1)S(1)}, bf16[128,3584]{1,0:T(8,128)(2,1)S(1)}, bf16[3584,512]{1,0:T(8,128)(2,1)S(1)}) custom-call(bf16[128,3584]{1,0:T(8,128)(2,1)} %hid.1, bf16[3584,512]{1,0:T(8,128)(2,1)} %wgt.1, bf16[128,512]{1,0:T(8,128)(2,1)} %ogr.1), custom_call_target="tpu_custom_call" | custom-call | tf_op jit(solution)/shard_map/rotated_projection/pallas_call | solution.py:315
  171.6 0.7 copy.9
  172.3 0.9 copy.10
  173.2 1.8 %copy.11 = bf16[3584,512]{1,0:T(8,128)(2,1)} copy(bf16[3584,512]{1,0:T(8,128)(2,1)S(1)} %get-tuple-element.5) | data formatting | bytes 7340032

commit v5 on v4

--- a/solution.py
+++ b/solution.py
@@ -272,6 +272,7 @@
         more = j + 1 < NB
         last = j + 1 == NB
         at(more, lambda: b2(j + 1))
+        at(jnp.logical_and(j >= 1, more), lambda: f2b(j + 1))
         at(j + 3 < NB, lambda: f1(j + 3))
         at(j == 0, lambda: b3a(j))
         at(j + 2 < NB, lambda: f2(j + 2))
@@ -279,13 +280,15 @@
         f4(j)
         at(more, lambda: b3(j))
         at(j + 3 < NB, lambda: b1(j + 3))
-        at(more, lambda: f2b(j + 1), lambda: f3(j + 1), lambda: b3a(j + 1))
+        at(j == 0, lambda: f2b(j + 1))
+        at(more, lambda: f3(j + 1), lambda: b3a(j + 1))
         at(jnp.logical_and(j >= 1, more), lambda: x2(j - 1))
         f5a(j)
         at(last, o1)
         f5b(j)
-        at(last, lambda: x2(j - 1), o2s)
+        at(last, lambda: x2(j - 1))
         b4(j)
+        at(last, o2s)
 
     x2(NB - 1)
 

time: 175 us -> 176 us (level)
  no operation moved by 1% of the time
where the time goes in v5:
time: 176 us
  Pallas kernels  172 us (98%)
  local copies, waits for them, and re-layouts  3.42 us (2%)
    pallas_call x1, Pallas kernels, body(): pl.pallas_call(kernel, name='rotated_projection', out_shape=(pltpu.VMEM((...  172 us

profile of v5, /device:TPU:1, one launch (start us, length us, event | category | flops | bytes accessed | tf_op | source)
XLA Modules:
  0.0 175.7 jit_solution(9100384979220733947)
XLA Ops:
  0.6 171.7 %rotated_projection.1 = (bf16[128,512]{1,0:T(8,128)(2,1)S(1)}, bf16[128,3584]{1,0:T(8,128)(2,1)S(1)}, bf16[3584,512]{1,0:T(8,128)(2,1)S(1)}) custom-call(bf16[128,3584]{1,0:T(8,128)(2,1)} %hid.1, bf16[3584,512]{1,0:T(8,128)(2,1)} %wgt.1, bf16[128,512]{1,0:T(8,128)(2,1)} %ogr.1), custom_call_target="tpu_custom_call" | custom-call | tf_op jit(solution)/shard_map/rotated_projection/pallas_call | solution.py:318
  172.3 0.7 copy.9
  173.0 0.9 copy.10
  173.9 1.8 %copy.11 = bf16[3584,512]{1,0:T(8,128)(2,1)} copy(bf16[3584,512]{1,0:T(8,128)(2,1)S(1)} %get-tuple-element.5) | data formatting | bytes 7340032
